TPU v7x, 32 devices: a whole 2x2x4 slice. The times are simulated.
32 devices in a mesh: dp: 8 (over z, x), tensor: 4 (over y, core).
Axes of the slice: x: 2, y: 2, z: 4, core: 2. Of those that a mesh axis runs over, the one named last changes fastest.
Arguments:
- bag_items: bfloat16 [16384, 64, 128], P('dp', 'tensor'), may hold values from -1.1953125 to 1.1953125
- bag_lengths: int32 [2048, 64], P('dp', 'tensor'), may hold values from 0 to 16, as said below
- send_counts: int32 [8, 8], P('dp'), may hold values from 0 to 48, as said below
- cross_weight: bfloat16 [1, 8192, 8192], P(None, 'tensor', 'dp'), may hold values from -0.0625 to 0.0625
- cross_bias: float32 [1, 8192], P(None, 'tensor'), may hold values from -3 to 3
Outputs:
- crossed: bfloat16 [2048, 8192], P('dp', 'tensor')
Inputs may be any that keep to these rules, and one draw needn't show every extreme that they name: `bag_lengths`: for every feature, the bags of the 256 rows of one aligned block hold 2048 items together; bags may be empty; in every aligned block and feature some bag holds exactly 16 items. `send_counts`: every row and every column sums to 256; each row has eight nonzero entries, one of them may be on the diagonal; no entry exceeds 48 and every row has an entry equal to 48.
All inputs are finite; a program needn't handle non-finite values.
Results may differ from a plain program's by a relative error of at most 0.0053.
Values may be sent and summed in bfloat16 or wider, within the bound.
No kernel may reach another device: no remote copies, remote signals or barrier semaphores. Data moves between devices by JAX's collectives and lax.ppermute only.
A program may use at most 128 MiB of HBM per device.

v0:
```python
import jax
import jax.numpy as jnp
from jax import lax
from jax.sharding import PartitionSpec as P

BAG = 8
CAP = 48


def shards(bag_items, bag_lengths, send_counts, cross_weight, cross_bias):
    row_count = bag_lengths.shape[0]
    feat_count = bag_lengths.shape[1]
    slot_count = bag_items.shape[0]
    embed_width = bag_items.shape[2]
    block_width = feat_count * embed_width
    bag_ends = jnp.cumsum(bag_lengths, axis=0)
    bag_starts = bag_ends - bag_lengths
    row_block = min(128, row_count)
    block_total = row_count // row_block
    window = min(slot_count, 2 * BAG * row_block)
    first_starts = bag_starts.reshape(block_total, row_block, feat_count)[:, 0, :]
    window_starts = jnp.clip(first_starts, 0, slot_count - window)
    feature_ids = jnp.arange(feat_count, dtype=jnp.int32)

    def take_window(start, feature):
        piece = lax.dynamic_slice(
            bag_items, (start, feature, jnp.int32(0)), (window, 1, embed_width)
        )
        return piece[:, 0, :]

    def pool_block(block_id):
        starts = window_starts[block_id]
        window_items = jax.vmap(take_window)(starts, feature_ids)
        row_first = (
            lax.dynamic_slice_in_dim(bag_starts, block_id * row_block, row_block, 0)
            - starts[None, :]
        )
        row_last = (
            lax.dynamic_slice_in_dim(bag_ends, block_id * row_block, row_block, 0) - starts[None, :]
        )
        positions = lax.broadcasted_iota(jnp.int32, (feat_count, row_block, window), 2)
        member = (positions >= row_first.T[:, :, None]) & (positions < row_last.T[:, :, None])
        one_hot = member.astype(jnp.bfloat16)
        return jnp.einsum("frs,fse->rfe", one_hot, window_items, preferred_element_type=jnp.float32)

    pooled_sum = lax.map(pool_block, jnp.arange(block_total, dtype=jnp.int32))
    pooled = pooled_sum.reshape(row_count, block_width).astype(jnp.bfloat16)
    device_count = lax.axis_size("dp")
    count_row = send_counts.reshape(-1)
    send_end = jnp.cumsum(count_row)
    send_start = send_end - count_row
    slot_ids = jnp.arange(CAP, dtype=jnp.int32)
    slot_index = jnp.minimum(send_start[:, None] + slot_ids[None, :], row_count - 1)
    slot_valid = slot_ids[None, :] < count_row[:, None]
    outgoing = jnp.where(slot_valid[:, :, None], pooled[slot_index], jnp.zeros((), jnp.bfloat16))
    received, recv_column = (
        lax.all_to_all(outgoing, "dp", split_axis=0, concat_axis=0, tiled=True),
        lax.all_to_all(
            count_row.reshape(device_count, 1), "dp", split_axis=0, concat_axis=0, tiled=True
        ),
    )
    recv_counts = recv_column.reshape(-1)
    recv_end = jnp.cumsum(recv_counts).astype(jnp.int32)
    recv_start = recv_end - recv_counts
    target_rows = jnp.arange(row_count, dtype=jnp.int32)
    source_block = jnp.sum((recv_end[None, :] <= target_rows[:, None]).astype(jnp.int32), axis=1)
    source_match = jnp.arange(device_count, dtype=jnp.int32)[None, :] == source_block[:, None]
    source_start = jnp.sum(jnp.where(source_match, recv_start[None, :], 0), axis=1)
    flat_index = source_block * CAP + target_rows - source_start
    cross_input = received.reshape(device_count * CAP, block_width)[flat_index]
    base_rows = cross_input.astype(jnp.float32)
    state = cross_input
    gathered = lax.all_gather(state, "tensor", axis=1, tiled=True)
    layer_weight = cross_weight[0]
    empty_sum = jnp.zeros((row_count, block_width), jnp.float32)
    w_piece = lax.all_gather(layer_weight, "dp", axis=1, tiled=True)
    columns = lax.slice_in_dim(gathered, 0, w_piece.shape[1], axis=1)
    product = empty_sum + lax.dot_general(
        columns, w_piece, (((1,), (1,)), ((), ())), preferred_element_type=jnp.float32
    )
    state = (base_rows * (product + cross_bias[0]) + state.astype(jnp.float32)).astype(jnp.bfloat16)
    return state


def solution(mesh):
    return jax.shard_map(
        shards,
        mesh=mesh,
        in_specs=(
            P("dp", "tensor", None),
            P("dp", "tensor"),
            P("dp", None),
            P(None, "tensor", "dp"),
            P(None, "tensor"),
        ),
        out_specs=P("dp", "tensor"),
        check_vma=False,
    )
```

profile of v0, /device:TPU:0, one launch (start us, length us, event | category | flops | bytes accessed | tf_op | source)
XLA Modules:
  0.0 814.9 jit_solution(1087858234139182849)
XLA Ops:
  6.5 1.3 copy.32
  7.9 7.3 all-to-all-start.1
  15.1 0.7 copy_bitcast_fusion.1
  15.8 0.6 reduce-window.25
  16.4 0.2 slice_reduce_fusion
  16.6 0.8 fusion.29
  17.5 0.1 copy.33
  17.6 12.3 %copy.30 = bf16[2048,16,128]{0,2,1:T(8,128)(2,1)} copy(bf16[2048,16,128]{2,1,0:T(8,128)(2,1)} %param.7) | data formatting | bytes 16777216
  29.9 37.9 %while.11 = (s32[]{:T(128)}, bf16[2,128,16,128]{1,3,2,0:T(8,128)(2,1)S(1)}, s32[2]{0:T(128)S(1)}, s32[2,16]{1,0:T(2,128)S(1)}, bf16[2048,16,128]{0,2,1:T(8,128)(...) while((s32[]{:T(128)}, ...), condition=%wide.region_3.4_spmd.clone, body=%wide.region_2.3_spmd.clone.sunk | while | flops 1086328960 | bytes 26264288 | solution.py:46
  29.9 0.6 dynamic_slice.31
  32.9 8.3 %gather_fusion = bf16[16,2048,128]{1,2,0:T(8,128)(2,1)} fusion(bf16[2048,16,128]{0,2,1:T(8,128)(2,1)} %get-tuple-element.190, s32[16]{0:T(128)S(1)} %fusion.40), kind=kCustom, calls=%fused_computation.clone.clone.1 | custom fusion | bytes 16777408 | tf_op jit(solution)/shard_map/while/body/eval_jaxpr/vmap()/gather | solution.py:26
  41.1 7.8 fusion.42
  48.9 0.6 dynamic_slice.31
  51.9 8.3 %gather_fusion = bf16[16,2048,128]{1,2,0:T(8,128)(2,1)} fusion(bf16[2048,16,128]{0,2,1:T(8,128)(2,1)} %get-tuple-element.190, s32[16]{0:T(128)S(1)} %fusion.40), kind=kCustom, calls=%fused_computation.clone.clone.1 | custom fusion | bytes 16777408 | tf_op jit(solution)/shard_map/while/body/eval_jaxpr/vmap()/gather | solution.py:26
  60.1 7.8 fusion.42
  67.9 1.0 copy.31
  68.9 0.3 copy.42
  69.2 0.2 reduce-window.27
  69.4 0.1 reshape.249
  69.6 2.4 gather_fusion.1
  72.0 1.3 broadcast_select_fusion
  73.4 6.0 all-to-all-start
  79.4 0.2 reduce.1
  79.7 0.2 reduce-window.28
  79.8 0.1 convert_reduce_fusion
  79.9 0.1 select_reduce_fusion
  80.0 35.8 %all-to-all-done = bf16[8,48,2048]{2,1,0:T(8,128)(2,1)S(1)} async-done(((bf16[8,48,2048]{2,1,0:T(8,128)(2,1)}), bf16[8,48,2048]{2,1,0:T(8,128)(2,1)S(1)}, u32[]{:S(2)}, u32[]{:S(2)}) %all-to-all-start) | async-done | bytes 1572896 | tf_op jit(solution)/shard_map/all_to_all | solution.py:57
  115.8 2.3 gather_fusion.2
  118.2 0.7 all-gather.7.cloned.1.call-update
  118.9 33.0 %all-gather.5.cloned.1.call-done = bf16[256,8192]{1,0:T(8,128)(2,1)} async-done(((bf16[256,2048]{1,0:T(8,128)(2,1)}), bf16[256,8192]{1,0:T(8,128)(2,1)}) %all-gather.5.cloned.1.call-update) | async-done | bytes 4194320 | tf_op jit(solution)/shard_map/all_gather | solution.py:73
  151.9 639.3 %all-gather.7.cloned.1.call-done = bf16[1,2048,8192]{2,1,0:T(8,128)(2,1)} async-done(((bf16[1,2048,1024]{2,1,0:T(8,128)(2,1)}), bf16[1,2048,8192]{2,1,0:T(8,128)(2,1)}) %all-gather.7.cloned.1.call-update) | async-done | bytes 33554448 | tf_op jit(solution)/shard_map/all_gather | solution.py:76
  791.2 16.8 %fusion.26 = bf16[256,2048]{1,0:T(8,128)(2,1)} fusion(bf16[256,8192]{1,0:T(8,128)(2,1)} %all-gather.5.cloned.1.call-done, bf16[1,2048,8192]{2,1,0:T(8,128)(2,1)} %all-gather.7.cloned.1.call-done, bf16[256,2048]{1,0:T(8,128)(2,1)S(1)} %copy-done, f32[2048]{0:T(1024)S(1)} %bitcast.99), kind=kOutput, calls=%fused_computation.27 | convolution fusion | flops 8592556032 | bytes 39854080 | tf_op jit(solution)/shard_map/dot_general | solution.py:78
  (31 shorter events, 0.6 us)
Async XLA Ops:
  7.9 65.5 %all-to-all-start.1 = ((s32[8,1,1]{2,1,0:T(1,128)}), s32[8,1,1]{2,1,0:T(1,128)S(1)}, u32[]{:S(2)}, u32[]{:S(2)}) async-start(s32[8,1,1]{2,1,0:T(1,128)} %copy.32), calls=%async_computation.1 | async-start | bytes 8192 | tf_op jit(solution)/shard_map/all_to_all | solution.py:58
  67.9 1.3 copy-start.1
  73.4 42.4 %all-to-all-start = ((bf16[8,48,2048]{2,1,0:T(8,128)(2,1)}), bf16[8,48,2048]{2,1,0:T(8,128)(2,1)S(1)}, u32[]{:S(2)}, u32[]{:S(2)}) async-start(bf16[8,48,2048]{2,1,0:T(8,128)(2,1)} %broadcast_select_fusion), calls=%async_computation | async-start | bytes 3145728 | tf_op jit(solution)/shard_map/all_to_all | solution.py:57
  79.4 72.5 %all-gather.5.cloned.1.call-start = ((), (), s32[]{:S(2)}) async-start(), calls=%async_computation.2 | async-start | bytes 5242880 | tf_op jit(solution)/shard_map/all_gather | solution.py:73
  118.1 673.1 %copy-start = (bf16[256,2048]{1,0:T(8,128)(2,1)S(1)}, bf16[256,2048]{1,0:T(8,128)(2,1)}, u32[]{:S(2)}) copy-start(bf16[256,2048]{1,0:T(8,128)(2,1)} %gather_fusion.2) | copy-start | bytes 3145732
  118.1 673.1 %copy-start.2 = (f32[1,2048]{1,0:T(1,128)S(1)}, f32[1,2048]{1,0:T(1,128)}, u32[]{:S(2)}) copy-start(f32[1,2048]{1,0:T(1,128)} %param.11) | copy-start | bytes 24580
  118.2 673.0 %all-gather.7.cloned.1.call-start = ((), (), s32[]{:S(2)}) async-start(), calls=%async_computation.3 | async-start | bytes 37748736 | tf_op jit(solution)/shard_map/all_gather | solution.py:76
Sparse Core Ops, SparseCore 0:
  118.3 33.5 all-gather.4
  153.4 637.7 all-gather.6
where the time goes:
time: 816 us; the launch traced here: 815 us
  waiting for transfers between devices  709 us (87%)
  local copies, waits for them, and re-layouts  38.4 us (5%)
  matrix products  32.3 us (4%)
  between operations  13.5 us (2%)
  starting transfers between devices  13.3 us (2%)
    all_gather x1, waiting for transfers between devices, shards(): w_piece = lax.all_gather(layer_weight, 'dp', axis=1, tiled=True)  639 us
    all_to_all x1, waiting for transfers between devices, shards(): lax.all_to_all(outgoing, 'dp', split_axis=0, concat_axis=0, tiled=True)  35.8 us
    all_gather x1, waiting for transfers between devices, shards(): gathered = lax.all_gather(state, 'tensor', axis=1, tiled=True)  33 us
    dot_general x1, matrix products, shards(): lax.dot_general(columns, w_piece, (((1,), (1,)), ((), ())), preferred_ele...  16.8 us
    gather x2, local copies, waits for them, and re-layouts, take_window(): lax.dynamic_slice(bag_items, (start, feature, jnp.int32(0)), (window, 1,...  16.5 us
  transfers between devices with their start and end apart: 4, of which 3 were waited for; matrix products, arithmetic and copies ran while one was open for 7% of the time, Pallas kernels for 0%

commit v1 on v0

--- a/solution.py
+++ b/solution.py
@@ -5,6 +5,19 @@
 
 BAG = 8
 CAP = 48
+
+
+def gather_around(x, axis, dim):
+    ways = lax.axis_size(axis)
+    up = [(d, (d + 1) % ways) for d in range(ways)]
+    down = [(d, (d - 1) % ways) for d in range(ways)]
+    earlier, later = ([x], [x])
+    for _ in range(ways // 2):
+        earlier.append(lax.ppermute(earlier[-1], axis, up))
+    for _ in range((ways - 1) // 2):
+        later.append(lax.ppermute(later[-1], axis, down))
+    line = jnp.concatenate([*earlier[::-1], *later[1:]], axis=dim)
+    return jnp.roll(line, (lax.axis_index(axis) - ways // 2) * x.shape[dim], axis=dim)
 
 
 def shards(bag_items, bag_lengths, send_counts, cross_weight, cross_bias):
@@ -73,7 +86,7 @@
     gathered = lax.all_gather(state, "tensor", axis=1, tiled=True)
     layer_weight = cross_weight[0]
     empty_sum = jnp.zeros((row_count, block_width), jnp.float32)
-    w_piece = lax.all_gather(layer_weight, "dp", axis=1, tiled=True)
+    w_piece = gather_around(layer_weight, "dp", 1)
     columns = lax.slice_in_dim(gathered, 0, w_piece.shape[1], axis=1)
     product = empty_sum + lax.dot_general(
         columns, w_piece, (((1,), (1,)), ((), ())), preferred_element_type=jnp.float32

time: 816 us -> 757 us (0.928)
  waiting for transfers between devices: 709 us -> 411 us
  starting transfers between devices: 13.3 us -> 184 us
  local copies, waits for them, and re-layouts: 38.4 us -> 105 us
    all_gather x1 -> x0, waiting for transfers between devices: 639 us -> none  [shards(): w_piece = lax.all_gather(layer_weight, 'dp', axis=1, tiled=True)]
    ppermute x0 -> x7, waiting for transfers between devices: none -> 318 us  [the longest x4 318 us: gather_around(): earlier.append(lax.ppermute(earlier[-1], axis, up))]
    ppermute x0 -> x7, starting transfers between devices: none -> 177 us  [the longest x3 169 us: gather_around(): later.append(lax.ppermute(later[-1], axis, down))]
    unnamed x9 -> x30, local copies, waits for them, and re-layouts: 12.7 us -> 75.1 us
    all_to_all x1, waiting for transfers between devices: 35.8 us -> 92.1 us  [shards(): lax.all_to_all(outgoing, 'dp', split_axis=0, concat_axis=0, tiled=True)]
    all_gather x1, waiting for transfers between devices: 33 us -> 0.01 us  [shards(): gathered = lax.all_gather(state, 'tensor', axis=1, tiled=True)]
  transfers between devices with their start and end apart: 4 -> 10, of which waited for: 3 -> 4; matrix products, arithmetic and copies ran while one was open for 7% -> 16% of each run, Pallas kernels for 0% -> 0%
where the time goes in v1:
time: 757 us; the launch traced here: 755 us
  waiting for transfers between devices  411 us (54%)
  starting transfers between devices  184 us (24%)
  local copies, waits for them, and re-layouts  105 us (14%)
  matrix products  32.7 us (4%)
  between operations  13.5 us (2%)
    ppermute x4, waiting for transfers between devices, gather_around(): earlier.append(lax.ppermute(earlier[-1], axis, up))  318 us
    ppermute x3, starting transfers between devices, gather_around(): later.append(lax.ppermute(later[-1], axis, down))  169 us
    all_to_all x1, waiting for transfers between devices, shards(): lax.all_to_all(outgoing, 'dp', split_axis=0, concat_axis=0, tiled=True)  92.1 us
    unnamed x30, local copies, waits for them, and re-layouts  75.1 us
    dot_general x1, matrix products, shards(): lax.dot_general(columns, w_piece, (((1,), (1,)), ((), ())), preferred_ele...  17.1 us
    gather x2, local copies, waits for them, and re-layouts, take_window(): lax.dynamic_slice(bag_items, (start, feature, jnp.int32(0)), (window, 1,...  16.5 us
    dot_general x2, matrix products, pool_block(): jnp.einsum('frs,fse->rfe', one_hot, window_items, preferred_element_type=...  15.5 us
  transfers between devices with their start and end apart: 10, of which 4 were waited for; matrix products, arithmetic and copies ran while one was open for 16% of the time, Pallas kernels for 0%

profile of v1, /device:TPU:0, one launch (start us, length us, event | category | flops | bytes accessed | tf_op | source)
XLA Modules:
  0.0 754.9 jit_solution(6641251169219438019)
XLA Ops:
  6.5 2.9 collective-permute-start
  9.5 93.8 %collective-permute-done = bf16[2048,1024]{1,0:T(8,128)(2,1)S(1)} collective-permute-done((bf16[2048,1024]{1,0:T(8,128)(2,1)}, bf16[2048,1024]{1,0:T(8,128)(2,1)S(1)}, u32[]{:S(2)}, u32[]{:S(2)}) %collective-permute-start) | collective-permute-done | bytes 4194336 | tf_op jit(solution)/shard_map/ppermute | solution.py:16
  105.2 4.7 collective-permute-start.4
  110.0 174.7 %collective-permute-done.1 = bf16[2048,1024]{1,0:T(8,128)(2,1)} collective-permute-done((bf16[2048,1024]{1,0:T(8,128)(2,1)S(1)}, bf16[2048,1024]{1,0:T(8,128)(2,1)}, u32[]{:S(2)}, u32[]{:S(2)}) %collective-permute-start.1) | collective-permute-done | bytes 4194336 | tf_op jit(solution)/shard_map/ppermute | solution.py:16
  284.7 2.6 collective-permute-start.2
  288.6 3.4 all-to-all-start.1
  294.4 12.3 %copy.30 = bf16[2048,16,128]{0,2,1:T(8,128)(2,1)} copy(bf16[2048,16,128]{2,1,0:T(8,128)(2,1)} %param.7) | data formatting | bytes 16777216
  306.8 71.4 %collective-permute-start.5 = (bf16[2048,1024]{1,0:T(8,128)(2,1)}, bf16[2048,1024]{1,0:T(8,128)(2,1)}, u32[]{:S(2)}, u32[]{:S(2)}) collective-permute-start(bf16[2048,1024]{1,0:T(8,128)(2,1)} %collective-permute-done.4), channel_id=1, source_target_pairs={{0,28},{4,0},{8,4},{12,8},{16,12},{20,16},{24,20},{28,24},{1,29},{... | collective-permute-start | bytes 12582920 | tf_op jit(solution)/shard_map/ppermute | solution.py:18
  378.2 37.9 %while.11 = (s32[]{:T(128)}, bf16[2,128,16,128]{1,3,2,0:T(8,128)(2,1)S(1)}, s32[2]{0:T(128)S(1)}, s32[2,16]{1,0:T(2,128)S(1)}, bf16[2048,16,128]{0,2,1:T(8,128)(...) while((s32[]{:T(128)}, ...), condition=%wide.region_3.4_spmd.clone, body=%wide.region_2.3_spmd.clone.sunk | while | flops 1086328960 | bytes 26264288 | solution.py:59
  381.1 8.3 %gather_fusion = bf16[16,2048,128]{1,2,0:T(8,128)(2,1)} fusion(bf16[2048,16,128]{0,2,1:T(8,128)(2,1)} %get-tuple-element.190, s32[16]{0:T(128)S(1)} %fusion.41), kind=kCustom, calls=%fused_computation.clone.clone.1 | custom fusion | bytes 16777408 | tf_op jit(solution)/shard_map/while/body/eval_jaxpr/vmap()/gather | solution.py:39
  389.4 7.8 %fusion.43 = bf16[2,128,16,128]{1,3,2,0:T(8,128)(2,1)S(1)} fusion(bf16[2,128,16,128]{1,3,2,0:T(8,128)(2,1)S(1)} %get-tuple-element.175, s32[]{:T(128)} %get-tuple-element.174, bf16[16,2048,128]{1,2,0:T(8,128)(2,1)} %gather_fusion, s32[16,128]{1,0:T(8,128)S(1)} %get-tuple-element.160, s32[16,128]{1,0:T(8,128)S(1)} %get-tuple-element.161), kind=kOutput, calls=%fused_computation.11.clone.1 | convolution fusion | flops 1086324736 | bytes 9453572 | tf_op jit(solution)/shard_map/while/body/eval_jaxpr/frs,fse->rfe/dot_general | solution.py:57
  400.1 8.3 %gather_fusion = bf16[16,2048,128]{1,2,0:T(8,128)(2,1)} fusion(bf16[2048,16,128]{0,2,1:T(8,128)(2,1)} %get-tuple-element.190, s32[16]{0:T(128)S(1)} %fusion.41), kind=kCustom, calls=%fused_computation.clone.clone.1 | custom fusion | bytes 16777408 | tf_op jit(solution)/shard_map/while/body/eval_jaxpr/vmap()/gather | solution.py:39
  408.4 7.8 %fusion.43 = bf16[2,128,16,128]{1,3,2,0:T(8,128)(2,1)S(1)} fusion(bf16[2,128,16,128]{1,3,2,0:T(8,128)(2,1)S(1)} %get-tuple-element.175, s32[]{:T(128)} %get-tuple-element.174, bf16[16,2048,128]{1,2,0:T(8,128)(2,1)} %gather_fusion, s32[16,128]{1,0:T(8,128)S(1)} %get-tuple-element.160, s32[16,128]{1,0:T(8,128)S(1)} %get-tuple-element.161), kind=kOutput, calls=%fused_computation.11.clone.1 | convolution fusion | flops 1086324736 | bytes 9453572 | tf_op jit(solution)/shard_map/while/body/eval_jaxpr/frs,fse->rfe/dot_general | solution.py:57
  416.3 49.8 %collective-permute-done.2 = bf16[2048,1024]{1,0:T(8,128)(2,1)} collective-permute-done((bf16[2048,1024]{1,0:T(8,128)(2,1)}, bf16[2048,1024]{1,0:T(8,128)(2,1)}, u32[]{:S(2)}, u32[]{:S(2)}) %collective-permute-start.2) | collective-permute-done | bytes 4194336 | tf_op jit(solution)/shard_map/ppermute | solution.py:16
  466.2 2.5 collective-permute-start.3
  470.1 2.5 gather_fusion.1
  473.9 3.6 all-to-all-start
  477.6 93.1 %collective-permute-start.6 = (bf16[2048,1024]{1,0:T(8,128)(2,1)}, bf16[2048,1024]{1,0:T(8,128)(2,1)}, u32[]{:S(2)}, u32[]{:S(2)}) collective-permute-start(bf16[2048,1024]{1,0:T(8,128)(2,1)} %collective-permute-done.5), channel_id=1, source_target_pairs={{0,28},{4,0},{8,4},{12,8},{16,12},{20,16},{24,20},{28,24},{1,29},{... | collective-permute-start | bytes 12582920 | tf_op jit(solution)/shard_map/ppermute | solution.py:18
  571.3 92.1 %all-to-all-done = bf16[8,48,2048]{2,1,0:T(8,128)(2,1)S(1)} async-done(((bf16[8,48,2048]{2,1,0:T(8,128)(2,1)}), bf16[8,48,2048]{2,1,0:T(8,128)(2,1)S(1)}, u32[]{:S(2)}, u32[]{:S(2)}) %all-to-all-start) | async-done | bytes 1572896 | tf_op jit(solution)/shard_map/all_to_all | solution.py:70
  665.8 4.6 constant_dynamic-update-slice_fusion.15
  670.4 4.7 constant_dynamic-update-slice_fusion.14
  675.1 5.2 constant_dynamic-update-slice_fusion.13
  685.0 4.6 constant_dynamic-update-slice_fusion.10
  689.6 4.6 constant_dynamic-update-slice_fusion.9
  694.1 4.6 constant_dynamic-update-slice_fusion.8
  698.7 4.6 constant_dynamic-update-slice_fusion.7
  703.3 4.6 constant_dynamic-update-slice_fusion.6
  707.8 4.6 constant_dynamic-update-slice_fusion.5
  717.1 4.5 constant_dynamic-update-slice_fusion.2
  721.7 4.6 constant_dynamic-update-slice_fusion.1
  726.3 4.6 constant_dynamic-update-slice_fusion
  730.9 17.1 %fusion.26 = bf16[256,2048]{1,0:T(8,128)(2,1)} fusion(bf16[256,8192]{1,0:T(8,128)(2,1)} %all-gather.3.cloned.1.call-done, bf16[2048,16384]{1,0:T(8,128)(2,1)} %constant_dynamic-update-slice_fusion, s32[]{:T(128)S(6)} %select_n.73, bf16[256,2048]{1,0:T(8,128)(2,1)S(1)} %copy-done.3, f32[2048]{0:T(1024)S(1)} %bitcast.95), kind=kOutput, calls=%fused_computation.27 | convolution fusion | flops 8592556032 | bytes 39854084 | tf_op jit(solution)/shard_map/dot_general | solution.py:91
  (64 shorter events, 22.6 us)
Async XLA Ops:
  6.5 96.8 %collective-permute-start = (bf16[2048,1024]{1,0:T(8,128)(2,1)}, bf16[2048,1024]{1,0:T(8,128)(2,1)S(1)}, u32[]{:S(2)}, u32[]{:S(2)}) collective-permute-start(bf16[2048,1024]{1,0:T(8,128)(2,1)} %bitcast.83), channel_id=1, source_target_pairs={{0,4},{4,8},{8,12},{12,16},{16,20},{20,24},{24,28},{28,0},{1,5},{5... | collective-permute-start | bytes 12582920 | tf_op jit(solution)/shard_map/ppermute | solution.py:16
  103.3 1.9 copy-start.1
  105.2 179.4 %collective-permute-start.1 = (bf16[2048,1024]{1,0:T(8,128)(2,1)S(1)}, bf16[2048,1024]{1,0:T(8,128)(2,1)}, u32[]{:S(2)}, u32[]{:S(2)}) collective-permute-start(bf16[2048,1024]{1,0:T(8,128)(2,1)S(1)} %collective-permute-done), channel_id=1, source_target_pairs={{0,4},{4,8},{8,12},{12,16},{16,20},{20,24},{24,28},{28,0},{1,5},{5... | collective-permute-start | bytes 12582920 | tf_op jit(solution)/shard_map/ppermute | solution.py:16
  105.2 201.6 %collective-permute-start.4 = (bf16[2048,1024]{1,0:T(8,128)(2,1)}, bf16[2048,1024]{1,0:T(8,128)(2,1)}, u32[]{:S(2)}, u32[]{:S(2)}) collective-permute-start(bf16[2048,1024]{1,0:T(8,128)(2,1)} %bitcast.84), channel_id=1, source_target_pairs={{0,28},{4,0},{8,4},{12,8},{16,12},{20,16},{24,20},{28,24},{1,29},{... | collective-permute-start | bytes 12582920 | tf_op jit(solution)/shard_map/ppermute | solution.py:18
  284.7 181.5 %collective-permute-start.2 = (bf16[2048,1024]{1,0:T(8,128)(2,1)}, bf16[2048,1024]{1,0:T(8,128)(2,1)}, u32[]{:S(2)}, u32[]{:S(2)}) collective-permute-start(bf16[2048,1024]{1,0:T(8,128)(2,1)} %collective-permute-done.1), channel_id=1, source_target_pairs={{0,4},{4,8},{8,12},{12,16},{16,20},{20,24},{24,28},{28,0},{1,5},{5... | collective-permute-start | bytes 12582920 | tf_op jit(solution)/shard_map/ppermute | solution.py:16
  288.6 185.4 %all-to-all-start.1 = ((s32[8,1,1]{2,1,0:T(1,128)}), s32[8,1,1]{2,1,0:T(1,128)S(1)}, u32[]{:S(2)}, u32[]{:S(2)}) async-start(s32[8,1,1]{2,1,0:T(1,128)} %copy.32), calls=%async_computation.1 | async-start | bytes 8192 | tf_op jit(solution)/shard_map/all_to_all | solution.py:71
  306.8 170.8 %collective-permute-start.5 = (bf16[2048,1024]{1,0:T(8,128)(2,1)}, bf16[2048,1024]{1,0:T(8,128)(2,1)}, u32[]{:S(2)}, u32[]{:S(2)}) collective-permute-start(bf16[2048,1024]{1,0:T(8,128)(2,1)} %collective-permute-done.4), channel_id=1, source_target_pairs={{0,28},{4,0},{8,4},{12,8},{16,12},{20,16},{24,20},{28,24},{1,29},{... | collective-permute-start | bytes 12582920 | tf_op jit(solution)/shard_map/ppermute | solution.py:18
  378.2 38.0 %copy-start.4 = (s32[1,8]{1,0:T(1,128)S(1)}, s32[1,8]{1,0:T(1,128)}, u32[]{:S(2)}) copy-start(s32[1,8]{1,0:T(1,128)} %param.9) | copy-start | bytes 100
  466.2 199.6 %collective-permute-start.3 = (bf16[2048,1024]{1,0:T(8,128)(2,1)}, bf16[2048,1024]{1,0:T(8,128)(2,1)}, u32[]{:S(2)}, u32[]{:S(2)}) collective-permute-start(bf16[2048,1024]{1,0:T(8,128)(2,1)} %collective-permute-done.2), channel_id=1, source_target_pairs={{0,4},{4,8},{8,12},{12,16},{16,20},{20,24},{24,28},{28,0},{1,5},{5... | collective-permute-start | bytes 12582920 | tf_op jit(solution)/shard_map/ppermute | solution.py:16
  473.9 189.5 %all-to-all-start = ((bf16[8,48,2048]{2,1,0:T(8,128)(2,1)}), bf16[8,48,2048]{2,1,0:T(8,128)(2,1)S(1)}, u32[]{:S(2)}, u32[]{:S(2)}) async-start(bf16[8,48,2048]{2,1,0:T(8,128)(2,1)} %broadcast_select_fusion), calls=%async_computation | async-start | bytes 3145728 | tf_op jit(solution)/shard_map/all_to_all | solution.py:70
  477.5 253.3 %all-gather.3.cloned.1.call-start = ((), (), s32[]{:S(2)}) async-start(), calls=%async_computation.2 | async-start | bytes 5242880 | tf_op jit(solution)/shard_map/all_gather | solution.py:86
  477.6 216.5 %collective-permute-start.6 = (bf16[2048,1024]{1,0:T(8,128)(2,1)}, bf16[2048,1024]{1,0:T(8,128)(2,1)}, u32[]{:S(2)}, u32[]{:S(2)}) collective-permute-start(bf16[2048,1024]{1,0:T(8,128)(2,1)} %collective-permute-done.5), channel_id=1, source_target_pairs={{0,28},{4,0},{8,4},{12,8},{16,12},{20,16},{24,20},{28,24},{1,29},{... | collective-permute-start | bytes 12582920 | tf_op jit(solution)/shard_map/ppermute | solution.py:18
  670.4 9.9 %copy-start.2 = (bf16[2048,1024]{1,0:T(8,128)(2,1)S(1)}, bf16[2048,1024]{1,0:T(8,128)(2,1)}, u32[]{:S(2)}) copy-start(bf16[2048,1024]{1,0:T(8,128)(2,1)} %copy-done.1) | copy-start | bytes 12582916
  675.1 7.5 copy-start
  721.7 9.2 %copy-start.3 = (bf16[256,2048]{1,0:T(8,128)(2,1)S(1)}, bf16[256,2048]{1,0:T(8,128)(2,1)}, u32[]{:S(2)}) copy-start(bf16[256,2048]{1,0:T(8,128)(2,1)} %gather_fusion.2) | copy-start | bytes 3145732
  721.7 9.2 %copy-start.5 = (f32[1,2048]{1,0:T(1,128)S(1)}, f32[1,2048]{1,0:T(1,128)}, u32[]{:S(2)}) copy-start(f32[1,2048]{1,0:T(1,128)} %param.11) | copy-start | bytes 24580
Sparse Core Ops, SparseCore 0:
  665.9 37.9 all-gather.2
